TPU v7x, 32 devices: a whole 2x2x4 slice. The times are simulated.
32 devices in a mesh: dp: 8 (over z, y), tensor: 4 (over x, core).
Axes of the slice: x: 2, y: 2, z: 4, core: 2. Of those that a mesh axis runs over, the one named last changes fastest.
Arguments:
- block_in: float32 [4096, 640], P(('dp', 'tensor')), may hold values from -6 to 6
- d_output: float32 [4096, 640], P(('dp', 'tensor')), may hold values from -6 to 6
- doc_ids: int32 [8, 512], P('dp'), may hold values from 0 to 3, never falling along the last dimension, each value on 1 to 256 neighbouring positions
- w_query: float32 [640, 1024], P('dp', 'tensor'), may hold values from -0.25 to 0.25
- w_key: float32 [640, 256], P('dp'), may hold values from -0.25 to 0.25
- w_value: float32 [640, 256], P('dp'), may hold values from -0.25 to 0.25
- w_output: float32 [640, 1024], P('dp', 'tensor'), may hold values from -0.1875 to 0.1875
- w_gate: float32 [640, 2048], P('dp', 'tensor'), may hold values from -0.25 to 0.25
- w_up: float32 [640, 2048], P('dp', 'tensor'), may hold values from -0.25 to 0.25
- w_down: float32 [640, 2048], P('dp', 'tensor'), may hold values from -0.125 to 0.125
- mom_query: float32 [640, 1024], P('dp', 'tensor'), may hold values from -112 to 112
- mom_key: float32 [640, 256], P('dp'), may hold values from -112 to 112
- mom_value: float32 [640, 256], P('dp'), may hold values from -112 to 112
- mom_output: float32 [640, 1024], P('dp', 'tensor'), may hold values from -112 to 112
- mom_gate: float32 [640, 2048], P('dp', 'tensor'), may hold values from -112 to 112
- mom_up: float32 [640, 2048], P('dp', 'tensor'), may hold values from -112 to 112
- mom_down: float32 [640, 2048], P('dp', 'tensor'), may hold values from -112 to 112
- gains: float32 [3072], replicated, may hold values from -0.4 to 0.6
- adam_first: float32 [3072], replicated, may hold values from -112 to 112
- adam_second: float32 [3072], replicated, may hold values from 204.8 to 8192
Outputs:
- block_out: float32 [4096, 640], P(('dp', 'tensor'))
- d_input: float32 [4096, 640], P(('dp', 'tensor'))
- grad_query: float32 [640, 1024], P('dp', 'tensor')
- grad_key: float32 [640, 256], P('dp')
- grad_value: float32 [640, 256], P('dp')
- grad_output: float32 [640, 1024], P('dp', 'tensor')
- grad_gate: float32 [640, 2048], P('dp', 'tensor')
- grad_up: float32 [640, 2048], P('dp', 'tensor')
- grad_down: float32 [640, 2048], P('dp', 'tensor')
- grad_gains: float32 [3072], replicated
- new_query: float32 [640, 1024], P('dp', 'tensor')
- new_key: float32 [640, 256], P('dp')
- new_value: float32 [640, 256], P('dp')
- new_output: float32 [640, 1024], P('dp', 'tensor')
- new_gate: float32 [640, 2048], P('dp', 'tensor')
- new_up: float32 [640, 2048], P('dp', 'tensor')
- new_down: float32 [640, 2048], P('dp', 'tensor')
- momentum_query: float32 [640, 1024], P('dp', 'tensor')
- momentum_key: float32 [640, 256], P('dp')
- momentum_value: float32 [640, 256], P('dp')
- momentum_output: float32 [640, 1024], P('dp', 'tensor')
- momentum_gate: float32 [640, 2048], P('dp', 'tensor')
- momentum_up: float32 [640, 2048], P('dp', 'tensor')
- momentum_down: float32 [640, 2048], P('dp', 'tensor')
- new_gains: float32 [3072], replicated
- next_first: float32 [3072], replicated
- next_second: float32 [3072], replicated
Inputs may be any that keep to these rules, and one draw needn't show every extreme that they name: `doc_ids`: along each sequence the document id never falls; each document covers 1 to half of 512 tokens, and some document covers exactly half of 512.
All inputs are finite; a program needn't handle non-finite values.
Results may differ from a plain program's by a relative error of at most 0.02.
Values may be sent and summed in bfloat16 or wider, within the bound.
No kernel may reach another device: no remote copies, remote signals or barrier semaphores. Data moves between devices by JAX's collectives and lax.ppermute only.
A program may use at most 64 MiB of HBM per device.

v0:
```python
import math
import jax
import jax.numpy as jnp
from jax import lax
from jax.sharding import PartitionSpec as P

NS_STEPS = 5
STEP = 5
EPSILON = 1e-06
ROPE_BASE = 10000.0
MUON_BETA = 0.95
MUON_RATE = 0.04
MUON_DECAY = 0.1
POLY_FIRST = 3.4445
POLY_SECOND = -4.775
POLY_THIRD = 2.0315
FIRST_DECAY = 0.9
SECOND_DECAY = 0.95
ADAM_RATE = 0.05
ADAM_EPSILON = 1e-08
MASKED = -1e30


def rms_norm(values, gain):
    factor = lax.rsqrt(jnp.mean(values * values, axis=-1, keepdims=True) + EPSILON)
    return values * factor * (1.0 + gain)


def rotate(values, cosine, sine):
    half = values.shape[-1] // 2
    turned = jnp.concatenate([-values[..., half:], values[..., :half]], axis=-1)
    return values * cosine + turned * sine


def head_map(raw, gain, cosine, sine):
    return rotate(rms_norm(raw, gain), cosine, sine)


def gated(gate, upper):
    return jax.nn.gelu(gate, approximate=True) * upper


def rope_tables(doc_rows, head_width):
    length = doc_rows.shape[-1]
    first = jnp.sum((doc_rows[..., None, :] < doc_rows[..., :, None]).astype(jnp.int32), axis=-1)
    offset = (jnp.arange(length, dtype=jnp.int32) - first).astype(jnp.float32)
    freqs = ROPE_BASE ** (-(2.0 * jnp.arange(head_width // 2, dtype=jnp.float32)) / head_width)
    angles = offset[..., None] * freqs
    angles = jnp.concatenate([angles, angles], axis=-1)
    return (jnp.cos(angles), jnp.sin(angles))


def gather_rows(values):
    return lax.all_gather(values, "tensor", axis=0, tiled=True)


def sum_rows(term, rows):
    return lax.psum_scatter(
        term(jnp.int32(0), rows * lax.axis_size("tensor")).astype(jnp.bfloat16),
        "tensor",
        scatter_dimension=0,
        tiled=True,
    ).astype(jnp.float32)


def gram_whole(matrix, share):
    gram_part = jnp.dot(matrix, matrix.T, preferred_element_type=jnp.float32) * share
    gram_rows = lax.psum_scatter(
        gram_part.astype(jnp.bfloat16), "tensor", scatter_dimension=0, tiled=True
    )
    return lax.all_gather(gram_rows, "tensor", axis=0, tiled=True)


def poly_step(ortho, square):
    once = jnp.dot(square, ortho, preferred_element_type=jnp.float32).astype(jnp.bfloat16)
    twice = jnp.dot(square, once, preferred_element_type=jnp.float32)
    mixed = (
        POLY_FIRST * ortho.astype(jnp.float32)
        + POLY_SECOND * once.astype(jnp.float32)
        + POLY_THIRD * twice
    )
    return mixed.astype(jnp.bfloat16)


def body(
    block_in,
    d_output,
    doc_ids,
    w_query,
    w_key,
    w_value,
    w_output,
    w_gate,
    w_up,
    w_down,
    mom_query,
    mom_key,
    mom_value,
    mom_output,
    mom_gate,
    mom_up,
    mom_down,
    gains,
    adam_first,
    adam_second,
):
    f32 = jnp.float32
    bf16 = jnp.bfloat16
    tensor_count = lax.axis_size("tensor")
    data_count = lax.axis_size("dp")
    local_rows = block_in.shape[0]
    model_width = block_in.shape[1]
    head_width = w_key.shape[1]
    local_heads = w_query.shape[1] // head_width
    seq_count = doc_ids.shape[0]
    seq_len = doc_ids.shape[1]
    total_rows = seq_count * seq_len
    scale = head_width ** (-0.5)
    pre_attn = gains[0:model_width]
    post_attn = gains[model_width : 2 * model_width]
    pre_ffn = gains[2 * model_width : 3 * model_width]
    post_ffn = gains[3 * model_width : 4 * model_width]
    gain_q = gains[4 * model_width : 4 * model_width + head_width]
    gain_k = gains[4 * model_width + head_width :]
    full_query, full_key, full_value, full_output, full_gate, full_up, full_down = (
        lax.all_gather(w_query.astype(bf16), "dp", axis=0, tiled=True),
        lax.all_gather(w_key.astype(bf16), "dp", axis=0, tiled=True),
        lax.all_gather(w_value.astype(bf16), "dp", axis=0, tiled=True),
        lax.all_gather(w_output.astype(bf16), "dp", axis=0, tiled=True),
        lax.all_gather(w_gate.astype(bf16), "dp", axis=0, tiled=True),
        lax.all_gather(w_up.astype(bf16), "dp", axis=0, tiled=True),
        lax.all_gather(w_down.astype(bf16), "dp", axis=0, tiled=True),
    )
    cosine, sine = rope_tables(doc_ids, head_width)
    places = jnp.arange(seq_len)
    allowed = (doc_ids[:, None, :] == doc_ids[:, :, None]) & (places[None, :] <= places[:, None])[
        None
    ]
    normed_one = gather_rows(rms_norm(block_in, pre_attn).astype(bf16))
    queries = jnp.dot(normed_one, full_query, preferred_element_type=f32).reshape(
        seq_count, seq_len, local_heads, head_width
    )
    keys = jnp.dot(normed_one, full_key, preferred_element_type=f32).reshape(
        seq_count, seq_len, head_width
    )
    values = (
        jnp.dot(normed_one, full_value, preferred_element_type=f32)
        .astype(bf16)
        .reshape(seq_count, seq_len, head_width)
    )
    query_rot = head_map(queries, gain_q, cosine[:, :, None, :], sine[:, :, None, :]).astype(bf16)
    key_rot = head_map(keys, gain_k, cosine, sine).astype(bf16)

    def masked_scores():
        raw = jnp.einsum("bshd,btd->bhst", query_rot, key_rot, preferred_element_type=f32) * scale
        return jnp.where(allowed[:, None], raw, MASKED)

    scores = masked_scores()
    top = jnp.max(scores, axis=-1, keepdims=True)
    log_total = top + jnp.log(jnp.sum(jnp.exp(scores - top), axis=-1, keepdims=True))
    probs = jnp.exp(scores - log_total).astype(bf16)
    heads = jnp.einsum("bhst,btd->bshd", probs, values, preferred_element_type=f32).astype(bf16)
    heads_flat = heads.reshape(total_rows, local_heads * head_width)

    def attn_term(start, count):
        return jnp.dot(heads_flat, full_output.T, preferred_element_type=f32)

    attn_local = sum_rows(attn_term, local_rows)
    middle = block_in + rms_norm(attn_local, post_attn)
    normed_two = gather_rows(rms_norm(middle, pre_ffn).astype(bf16))
    gate = jnp.dot(normed_two, full_gate, preferred_element_type=f32)
    upper = jnp.dot(normed_two, full_up, preferred_element_type=f32)
    hidden = gated(gate, upper).astype(bf16)

    def branch_term(start, count):
        return jnp.dot(hidden, full_down.T, preferred_element_type=f32)

    branch_local = sum_rows(branch_term, local_rows)
    block_out = middle + rms_norm(branch_local, post_ffn)
    pull = jax.vjp(rms_norm, branch_local, post_ffn)[1]
    d_branch_local, g_post_ffn = pull(d_output)
    branch_low = gather_rows(d_branch_local.astype(bf16))
    grad_down_part = jnp.einsum("rd,rf->df", branch_low, hidden, preferred_element_type=f32)
    d_hidden = jnp.dot(branch_low, full_down, preferred_element_type=f32)
    pull = jax.vjp(gated, gate, upper)[1]
    d_gate, d_upper = pull(d_hidden)
    gate_low = d_gate.astype(bf16)
    upper_low = d_upper.astype(bf16)
    grad_gate_part = jnp.einsum("rd,rf->df", normed_two, gate_low, preferred_element_type=f32)
    grad_up_part = jnp.einsum("rd,rf->df", normed_two, upper_low, preferred_element_type=f32)

    def hidden_term(start, count):
        first_part = jnp.dot(gate_low, full_gate.T, preferred_element_type=f32)
        return first_part + jnp.dot(upper_low, full_up.T, preferred_element_type=f32)

    d_normed_two = sum_rows(hidden_term, local_rows)
    pull = jax.vjp(rms_norm, middle, pre_ffn)[1]
    d_mid_extra, g_pre_ffn = pull(d_normed_two)
    d_middle = d_output + d_mid_extra
    pull = jax.vjp(rms_norm, attn_local, post_attn)[1]
    d_attn_local, g_post_attn = pull(d_middle)
    attn_low = gather_rows(d_attn_local.astype(bf16))
    grad_output_part = jnp.einsum("rd,re->de", attn_low, heads_flat, preferred_element_type=f32)
    d_heads = jnp.dot(attn_low, full_output, preferred_element_type=f32).astype(bf16)
    d_heads = d_heads.reshape(seq_count, seq_len, local_heads, head_width)
    prob_full = jnp.exp(masked_scores() - log_total)
    delta = jnp.einsum("bshd,bshd->bhs", d_heads, heads, preferred_element_type=f32)
    d_probs = jnp.einsum("bshd,btd->bhst", d_heads, values, preferred_element_type=f32)
    d_scores = (prob_full * (d_probs - delta[..., None]) * scale).astype(bf16)
    d_qrot = jnp.einsum("bhst,btd->bshd", d_scores, key_rot, preferred_element_type=f32)
    d_krot = jnp.einsum("bhst,bshd->bthd", d_scores, query_rot, preferred_element_type=f32)
    d_vals = jnp.einsum("bhst,bshd->bthd", probs, d_heads, preferred_element_type=f32)
    pull = jax.vjp(
        lambda raw, gain: head_map(raw, gain, cosine[:, :, None, :], sine[:, :, None, :]),
        queries,
        gain_q,
    )[1]
    d_queries, g_query = pull(d_qrot)
    pull = jax.vjp(lambda raw, gain: head_map(raw, gain, cosine, sine), keys, gain_k)[1]
    d_keys, g_key_heads = jax.vmap(pull, in_axes=2, out_axes=(2, 0))(d_krot)
    g_key = jnp.sum(g_key_heads, axis=0)
    query_low = d_queries.reshape(total_rows, local_heads * head_width).astype(bf16)
    key_low = d_keys.reshape(total_rows, local_heads, head_width).astype(bf16)
    value_low = d_vals.reshape(total_rows, local_heads, head_width).astype(bf16)
    grad_query_part = jnp.einsum("rd,re->de", normed_one, query_low, preferred_element_type=f32)
    grad_key_part = jnp.einsum("rd,rhe->de", normed_one, key_low, preferred_element_type=f32)
    grad_value_part = jnp.einsum("rd,rhe->de", normed_one, value_low, preferred_element_type=f32)

    def query_term(start, count):
        first_part = jnp.dot(query_low, full_query.T, preferred_element_type=f32)
        second_part = jnp.einsum("rhe,de->rd", key_low, full_key, preferred_element_type=f32)
        third_part = jnp.einsum("rhe,de->rd", value_low, full_value, preferred_element_type=f32)
        return first_part + second_part + third_part

    d_normed_one = sum_rows(query_term, local_rows)
    pull = jax.vjp(rms_norm, block_in, pre_attn)[1]
    d_in_extra, g_pre_attn = pull(d_normed_one)
    d_input = d_middle + d_in_extra
    gain_term = jnp.concatenate([g_pre_attn, g_post_attn, g_pre_ffn, g_post_ffn, g_query, g_key])
    sum_query, sum_output, sum_gate, sum_up, sum_down = (
        lax.psum_scatter(grad_query_part, "dp", scatter_dimension=0, tiled=True),
        lax.psum_scatter(grad_output_part, "dp", scatter_dimension=0, tiled=True),
        lax.psum_scatter(grad_gate_part, "dp", scatter_dimension=0, tiled=True),
        lax.psum_scatter(grad_up_part, "dp", scatter_dimension=0, tiled=True),
        lax.psum_scatter(grad_down_part, "dp", scatter_dimension=0, tiled=True),
    )
    key_total, value_total, grad_gains = lax.psum(
        (grad_key_part, grad_value_part, gain_term), ("dp", "tensor")
    )
    shard_rows = w_key.shape[0]
    my_data = lax.axis_index("dp")
    sum_key = lax.dynamic_slice_in_dim(key_total, my_data * shard_rows, shard_rows, 0)
    sum_value = lax.dynamic_slice_in_dim(value_total, my_data * shard_rows, shard_rows, 0)
    weights = (w_query, w_key, w_value, w_output, w_gate, w_up, w_down)
    moments = (mom_query, mom_key, mom_value, mom_output, mom_gate, mom_up, mom_down)
    reduced = (sum_query, sum_key, sum_value, sum_output, sum_gate, sum_up, sum_down)
    whole_cols = [
        weights[index].shape[1] * (1 if index in (1, 2) else tensor_count) for index in range(7)
    ]
    slot = max([weight.shape[1] for weight in weights])
    owners = [index * data_count // 7 for index in range(7)]
    moved = [MUON_BETA * moments[index] + reduced[index] for index in range(7)]
    outgoing = jnp.zeros((data_count, shard_rows, slot), bf16)
    for index in range(7):
        push = (reduced[index] + MUON_BETA * moved[index]).astype(bf16)
        padded = jnp.pad(push, ((0, 0), (0, slot - push.shape[1])))
        outgoing = outgoing.at[owners[index]].set(padded)
    arrived = lax.all_to_all(outgoing, "dp", split_axis=0, concat_axis=0, tiled=True)
    owned = arrived.reshape(data_count * shard_rows, slot)
    shared = (my_data == owners[1]) | (my_data == owners[2])
    share = jnp.where(shared, 1.0 / tensor_count, 1.0).astype(f32)
    owned_wide = owned.astype(f32)
    raw_square = gram_whole(owned, share)
    norm_total = jnp.sum(jnp.diagonal(raw_square).astype(f32))
    ortho = (owned_wide / (jnp.sqrt(norm_total) + 1e-07)).astype(bf16)
    for index in range(NS_STEPS):
        square = gram_whole(ortho, share)
        ortho = poly_step(ortho, square)
    returned = lax.all_to_all(
        ortho.reshape(data_count, shard_rows, slot), "dp", split_axis=0, concat_axis=0, tiled=True
    )
    updated = []
    for index in range(7):
        weight = weights[index]
        update = returned[owners[index], :, : weight.shape[1]].astype(f32)
        factor = 0.2 * math.sqrt(max(model_width, whole_cols[index]))
        updated.append(weight - MUON_RATE * (factor * update + MUON_DECAY * weight))
    next_first = FIRST_DECAY * adam_first + (1.0 - FIRST_DECAY) * grad_gains
    next_second = SECOND_DECAY * adam_second + (1.0 - SECOND_DECAY) * grad_gains * grad_gains
    first_fix = 1.0 - FIRST_DECAY**STEP
    second_fix = 1.0 - SECOND_DECAY**STEP
    new_gains = gains - ADAM_RATE * (next_first / first_fix) / (
        jnp.sqrt(next_second / second_fix) + ADAM_EPSILON
    )
    return (
        block_out,
        d_input,
        sum_query,
        sum_key,
        sum_value,
        sum_output,
        sum_gate,
        sum_up,
        sum_down,
        grad_gains,
        updated[0],
        updated[1],
        updated[2],
        updated[3],
        updated[4],
        updated[5],
        updated[6],
        moved[0],
        moved[1],
        moved[2],
        moved[3],
        moved[4],
        moved[5],
        moved[6],
        new_gains,
        next_first,
        next_second,
    )


def solution(mesh):
    return jax.shard_map(
        body,
        mesh=mesh,
        in_specs=(
            P(("dp", "tensor"), None),
            P(("dp", "tensor"), None),
            P("dp", None),
            P("dp", "tensor"),
            P("dp", None),
            P("dp", None),
            P("dp", "tensor"),
            P("dp", "tensor"),
            P("dp", "tensor"),
            P("dp", "tensor"),
            P("dp", "tensor"),
            P("dp", None),
            P("dp", None),
            P("dp", "tensor"),
            P("dp", "tensor"),
            P("dp", "tensor"),
            P("dp", "tensor"),
            P(),
            P(),
            P(),
        ),
        out_specs=(
            P(("dp", "tensor"), None),
            P(("dp", "tensor"), None),
            P("dp", "tensor"),
            P("dp", None),
            P("dp", None),
            P("dp", "tensor"),
            P("dp", "tensor"),
            P("dp", "tensor"),
            P("dp", "tensor"),
            P(),
            P("dp", "tensor"),
            P("dp", None),
            P("dp", None),
            P("dp", "tensor"),
            P("dp", "tensor"),
            P("dp", "tensor"),
            P("dp", "tensor"),
            P("dp", "tensor"),
            P("dp", None),
            P("dp", None),
            P("dp", "tensor"),
            P("dp", "tensor"),
            P("dp", "tensor"),
            P("dp", "tensor"),
            P(),
            P(),
            P(),
        ),
        check_vma=False,
    )
```

profile of v0, /device:TPU:0, one launch (start us, length us, event | category | flops | bytes accessed | tf_op | source)
XLA Modules:
  0.0 1146.8 jit_solution(16319865074403344235)
XLA Ops:
  11.0 9.4 all_gather.51
  20.4 31.4 %all_gather.53 = bf16[640,256]{1,0:T(8,128)(2,1)S(1)} all-gather(bf16[80,256]{1,0:T(8,128)(2,1)S(1)} %convert_element_type.303), channel_id=1, replica_groups=mesh['dp'=8,'tensor'=4] {'dp'}, dimensions={0}, use_global_device_ids=true | all-gather | bytes 368640 | tf_op jit(solution)/shard_map/all_gather | solution.py:127
  53.1 30.8 %all_gather.54 = bf16[640,256]{1,0:T(8,128)(2,1)S(1)} all-gather(bf16[80,256]{1,0:T(8,128)(2,1)S(1)} %convert_element_type.307), channel_id=1, replica_groups=mesh['dp'=8,'tensor'=4] {'dp'}, dimensions={0}, use_global_device_ids=true | all-gather | bytes 368640 | tf_op jit(solution)/shard_map/all_gather | solution.py:126
  86.3 2.5 fusion.43
  89.8 31.0 %all_gather.52 = bf16[640,256]{1,0:T(8,128)(2,1)S(1)} all-gather(bf16[80,256]{1,0:T(8,128)(2,1)S(1)} %convert_element_type.301), channel_id=1, replica_groups=mesh['dp'=8,'tensor'=4] {'dp'}, dimensions={0}, use_global_device_ids=true | all-gather | bytes 368640 | tf_op jit(solution)/shard_map/all_gather | solution.py:128
  121.5 31.3 %all_gather.55 = bf16[640,256]{1,0:T(8,128)(2,1)S(1)} all-gather(bf16[80,256]{1,0:T(8,128)(2,1)S(1)} %convert_element_type.313), channel_id=1, replica_groups=mesh['dp'=8,'tensor'=4] {'dp'}, dimensions={0}, use_global_device_ids=true | all-gather | bytes 368640 | tf_op jit(solution)/shard_map/all_gather | solution.py:129
  157.4 34.0 %all_gather.57 = bf16[640,512]{1,0:T(8,128)(2,1)} all-gather(bf16[80,512]{1,0:T(8,128)(2,1)S(1)} %convert_element_type.317), channel_id=1, replica_groups=mesh['dp'=8,'tensor'=4] {'dp'}, dimensions={0}, use_global_device_ids=true | all-gather | bytes 737280 | tf_op jit(solution)/shard_map/all_gather | solution.py:130
  191.3 33.8 %all_gather.58 = bf16[640,512]{1,0:T(8,128)(2,1)} all-gather(bf16[80,512]{1,0:T(8,128)(2,1)S(1)} %convert_element_type.318), channel_id=1, replica_groups=mesh['dp'=8,'tensor'=4] {'dp'}, dimensions={0}, use_global_device_ids=true | all-gather | bytes 737280 | tf_op jit(solution)/shard_map/all_gather | solution.py:131
  225.1 33.4 %all_gather.59 = bf16[640,512]{1,0:T(8,128)(2,1)} all-gather(bf16[80,512]{1,0:T(8,128)(2,1)S(1)} %convert_element_type.320), channel_id=1, replica_groups=mesh['dp'=8,'tensor'=4] {'dp'}, dimensions={0}, use_global_device_ids=true | all-gather | bytes 737280 | tf_op jit(solution)/shard_map/all_gather | solution.py:132
  261.6 7.4 all_gather.56
  270.1 1.7 multiply_convert_fusion.7
  272.6 1.5 convolution_convert_fusion.6
  274.1 23.2 %reduce-scatter.18.cloned.1.call-done = bf16[128,640]{1,0:T(8,128)(2,1)} async-done(((bf16[512,640]{1,0:T(8,128)(2,1)}), bf16[128,640]{1,0:T(8,128)(2,1)}) %reduce-scatter.18.cloned.1.call-update) | async-done | bytes 163856 | tf_op jit(solution)/shard_map/reduce_scatter | solution.py:58
  300.8 7.3 all_gather.60
  308.2 2.7 multiply_convert_fusion.6
  313.9 23.1 %reduce-scatter.20.cloned.1.call-done = bf16[128,640]{1,0:T(8,128)(2,1)} async-done(((bf16[512,640]{1,0:T(8,128)(2,1)}), bf16[128,640]{1,0:T(8,128)(2,1)}) %reduce-scatter.20.cloned.1.call-update) | async-done | bytes 163856 | tf_op jit(solution)/shard_map/reduce_scatter | solution.py:58
  338.9 2.3 fusion.71
  342.0 7.5 all_gather.61
  352.5 1.9 copy.50
  354.4 2.3 fusion.130
  357.7 1.9 fusion.55
  359.7 2.2 fusion.56
  363.3 3.5 fusion.49
  368.0 3.6 fusion.57
  374.5 1.7 fusion.132
  376.3 1.6 fusion.133
  378.1 1.6 fusion.134
  379.7 120.8 %all-reduce.12.cloned.1.call-done = (f32[640,256]{1,0:T(8,128)}, f32[640,256]{1,0:T(8,128)}) async-done(((f32[640,256]{1,0:T(8,128)}, f32[640,256]{1,0:T(8,128)}), (f32[640,256]{1,0:T(8,128)}, f32[640,256]{1,0:T(8,128)})) %all-reduce.12.cloned.1.call-update) | async-done | bytes 1310736 | tf_op jit(solution)/shard_map/psum | solution.py:247
  500.5 1.7 add_convert_fusion.4
  502.2 63.7 %reduce-scatter.24.cloned.1.call-done = f32[80,256]{1,0:T(8,128)} async-done(((f32[640,256]{1,0:T(8,128)}), f32[80,256]{1,0:T(8,128)}) %reduce-scatter.24.cloned.1.call-update) | async-done | bytes 81936 | tf_op jit(solution)/shard_map/reduce_scatter | solution.py:241
  565.9 1.5 add_convert_fusion.6
  569.7 61.8 %reduce-scatter.26.cloned.1.call-done = f32[80,256]{1,0:T(8,128)} async-done(((f32[640,256]{1,0:T(8,128)}), f32[80,256]{1,0:T(8,128)}) %reduce-scatter.26.cloned.1.call-update) | async-done | bytes 81936 | tf_op jit(solution)/shard_map/reduce_scatter | solution.py:242
  631.4 1.5 add_convert_fusion.3
  633.6 65.9 %reduce-scatter.28.cloned.1.call-done = f32[80,512]{1,0:T(8,128)} async-done(((f32[640,512]{1,0:T(8,128)}), f32[80,512]{1,0:T(8,128)}) %reduce-scatter.28.cloned.1.call-update) | async-done | bytes 163856 | tf_op jit(solution)/shard_map/reduce_scatter | solution.py:243
  699.6 1.6 fusion.97
  701.2 66.3 %reduce-scatter.30.cloned.1.call-done = f32[80,512]{1,0:T(8,128)} async-done(((f32[640,512]{1,0:T(8,128)}), f32[80,512]{1,0:T(8,128)}) %reduce-scatter.30.cloned.1.call-update) | async-done | bytes 163856 | tf_op jit(solution)/shard_map/reduce_scatter | solution.py:244
  767.5 1.6 fusion.99
  769.2 66.4 %reduce-scatter.32.cloned.1.call-done = f32[80,512]{1,0:T(8,128)} async-done(((f32[640,512]{1,0:T(8,128)}), f32[80,512]{1,0:T(8,128)}) %reduce-scatter.32.cloned.1.call-update) | async-done | bytes 163856 | tf_op jit(solution)/shard_map/reduce_scatter | solution.py:245
  835.6 1.6 fusion.101
  837.2 3.6 all-to-all-start
  840.9 15.5 %all-to-all-done = bf16[8,80,512]{2,1,0:T(8,128)(2,1)S(1)} async-done(((bf16[8,80,512]{2,1,0:T(8,128)(2,1)}), bf16[8,80,512]{2,1,0:T(8,128)(2,1)S(1)}, u32[]{:S(2)}, u32[]{:S(2)}) %all-to-all-start) | async-done | bytes 655392 | tf_op jit(solution)/shard_map/all_to_all | solution.py:268
  856.3 1.6 multiply_convert_fusion.5
  858.0 22.6 %reduce-scatter.34.cloned.1.call-done = bf16[160,640]{1,0:T(8,128)(2,1)} async-done(((bf16[640,640]{1,0:T(8,128)(2,1)}), bf16[160,640]{1,0:T(8,128)(2,1)}) %reduce-scatter.34.cloned.1.call-update) | async-done | bytes 204816 | tf_op jit(solution)/shard_map/reduce_scatter | solution.py:68
  880.6 8.4 all_gather.62
  889.0 5.8 gather_fusion
  896.2 1.6 multiply_convert_fusion.4
  898.0 23.9 %reduce-scatter.36.cloned.1.call-done = bf16[160,640]{1,0:T(8,128)(2,1)} async-done(((bf16[640,640]{1,0:T(8,128)(2,1)}), bf16[160,640]{1,0:T(8,128)(2,1)}) %reduce-scatter.36.cloned.1.call-update) | async-done | bytes 204816 | tf_op jit(solution)/shard_map/reduce_scatter | solution.py:68
  921.9 8.6 all_gather.63
  932.0 1.6 multiply_convert_fusion.3
  933.6 24.1 %reduce-scatter.38.cloned.1.call-done = bf16[160,640]{1,0:T(8,128)(2,1)} async-done(((bf16[640,640]{1,0:T(8,128)(2,1)}), bf16[160,640]{1,0:T(8,128)(2,1)}) %reduce-scatter.38.cloned.1.call-update) | async-done | bytes 204816 | tf_op jit(solution)/shard_map/reduce_scatter | solution.py:68
  957.7 8.4 all_gather.64
  967.6 1.6 multiply_convert_fusion.2
  969.2 24.1 %reduce-scatter.40.cloned.1.call-done = bf16[160,640]{1,0:T(8,128)(2,1)} async-done(((bf16[640,640]{1,0:T(8,128)(2,1)}), bf16[160,640]{1,0:T(8,128)(2,1)}) %reduce-scatter.40.cloned.1.call-update) | async-done | bytes 204816 | tf_op jit(solution)/shard_map/reduce_scatter | solution.py:68
  993.3 8.4 all_gather.65
  1003.2 1.6 multiply_convert_fusion.1
  1008.1 20.8 %reduce-scatter.42.cloned.1.call-done = bf16[160,640]{1,0:T(8,128)(2,1)} async-done(((bf16[640,640]{1,0:T(8,128)(2,1)}), bf16[160,640]{1,0:T(8,128)(2,1)}) %reduce-scatter.42.cloned.1.call-update) | async-done | bytes 204816 | tf_op jit(solution)/shard_map/reduce_scatter | solution.py:68
  1028.9 8.4 all_gather.66
  1038.8 1.6 multiply_convert_fusion
  1040.4 13.3 %reduce-scatter.22.cloned.1.call-done = bf16[128,640]{1,0:T(8,128)(2,1)} async-done(((bf16[512,640]{1,0:T(8,128)(2,1)}), bf16[128,640]{1,0:T(8,128)(2,1)}) %reduce-scatter.22.cloned.1.call-update) | async-done | bytes 163856 | tf_op jit(solution)/shard_map/reduce_scatter | solution.py:58
  1054.8 24.8 %reduce-scatter.44.cloned.1.call-done = bf16[160,640]{1,0:T(8,128)(2,1)} async-done(((bf16[640,640]{1,0:T(8,128)(2,1)}), bf16[160,640]{1,0:T(8,128)(2,1)}) %reduce-scatter.44.cloned.1.call-update) | async-done | bytes 204816 | tf_op jit(solution)/shard_map/reduce_scatter | solution.py:68
  1079.6 8.4 all_gather.67
  1088.7 1.6 fusion.12
  1090.4 5.7 all-to-all-start.1
  1096.1 41.0 %psum.23 = f32[3072]{0:T(1024)S(1)} all-reduce(f32[3072]{0:T(1024)S(1)} %constant_dynamic-update-slice_fusion), channel_id=1, replica_groups=mesh['dp'=8,'tensor'=4] {'dp','tensor'}, use_global_device_ids=true, to_apply=%region_32.33 | all-reduce | flops 3072 | bytes 24576 | tf_op jit(solution)/shard_map/psum | solution.py:247
  (286 shorter events, 55.3 us)
Async XLA Ops:
  7.2 13.2 %copy-start.56 = (f32[80,256]{1,0:T(8,128)S(1)}, f32[80,256]{1,0:T(8,128)}, u32[]{:S(2)}) copy-start(f32[80,256]{1,0:T(8,128)} %param.38) | copy-start | bytes 245764
  7.2 251.3 %reduce-scatter.16.cloned.1.call-start = ((), (), s32[]{:S(2)}) async-start(), calls=%async_computation.17 | async-start | bytes 819200 | tf_op jit(solution)/shard_map/reduce_scatter | solution.py:58
  9.9 42.3 %copy-start.75 = (f32[128]{0:T(128)}, f32[128]{0:T(128)S(1)}, u32[]{:S(2)}) copy-start(f32[128]{0:T(128)S(1)} %multiply_reduce_fusion.4) | copy-start | bytes 1540
  89.2 31.9 %copy-start.58 = (f32[80,256]{1,0:T(8,128)S(1)}, f32[80,256]{1,0:T(8,128)}, u32[]{:S(2)}) copy-start(f32[80,256]{1,0:T(8,128)} %param.40) | copy-start | bytes 245764
  121.2 31.6 %copy-start.30 = (bf16[512,256]{1,0:T(8,128)(2,1)}, bf16[512,256]{1,0:T(8,128)(2,1)S(1)}, u32[]{:S(2)}) copy-start(bf16[512,256]{1,0:T(8,128)(2,1)S(1)} %convolution_convert_fusion.10) | copy-start | bytes 786436
  153.1 2.3 copy-start.9
  154.5 142.8 %reduce-scatter.18.cloned.1.call-start = ((), (), s32[]{:S(2)}) async-start(), calls=%async_computation.18 | async-start | bytes 819200 | tf_op jit(solution)/shard_map/reduce_scatter | solution.py:58
  156.4 103.2 %copy-start = (f32[128,640]{1,0:T(8,128)S(1)}, f32[128,640]{1,0:T(8,128)}, u32[]{:S(2)}) copy-start(f32[128,640]{1,0:T(8,128)} %param.34) | copy-start | bytes 983044
  258.5 10.5 copy-start.4
  259.6 10.0 copy-start.77
  260.8 8.8 copy-start.78
  260.8 76.2 %copy-start.72 = (f32[128]{0:T(128)}, f32[128]{0:T(128)S(1)}, u32[]{:S(2)}) copy-start(f32[128]{0:T(128)S(1)} %fusion.115) | copy-start | bytes 1540
  270.1 2.5 copy-start.45
  274.0 62.9 %reduce-scatter.20.cloned.1.call-start = ((), (), s32[]{:S(2)}) async-start(), calls=%async_computation.19 | async-start | bytes 819200 | tf_op jit(solution)/shard_map/reduce_scatter | solution.py:58
  297.3 10.9 copy-start.41
  297.3 10.9 copy-start.46
  298.4 12.4 %copy-start.73 = (f32[128]{0:T(128)}, f32[128]{0:T(128)S(1)}, u32[]{:S(2)}) copy-start(f32[128]{0:T(128)S(1)} %fusion.116) | copy-start | bytes 1540
  308.1 2.7 copy-start.25
  308.2 2.7 copy-start.5
  313.8 186.7 %all-reduce.12.cloned.1.call-start = ((), (), s32[]{:S(2)}) async-start(), calls=%async_computation.32 | async-start | bytes 2621440 | tf_op jit(solution)/shard_map/psum | solution.py:247
  336.9 4.9 copy-start.24
  338.9 11.5 %copy-start.21 = (bf16[640,256]{1,0:T(8,128)(2,1)S(1)}, bf16[640,256]{1,0:T(8,128)(2,1)}, u32[]{:S(2)}) copy-start(bf16[640,256]{1,0:T(8,128)(2,1)} %copy-done.20) | copy-start | bytes 983044
  354.4 2.3 copy-start.10
  354.4 2.3 copy-start.36
  354.4 2.4 copy-start.13
  354.4 2.4 copy-start.31
  357.2 2.5 copy-start.7
  367.7 198.2 %reduce-scatter.24.cloned.1.call-start = ((), (), s32[]{:S(2)}) async-start(), calls=%async_computation.21 | async-start | bytes 737280 | tf_op jit(solution)/shard_map/reduce_scatter | solution.py:241
  373.1 258.3 %reduce-scatter.26.cloned.1.call-start = ((), (), s32[]{:S(2)}) async-start(), calls=%async_computation.22 | async-start | bytes 737280 | tf_op jit(solution)/shard_map/reduce_scatter | solution.py:242
  374.5 1.9 copy-start.38
  374.5 325.1 %reduce-scatter.28.cloned.1.call-start = ((), (), s32[]{:S(2)}) async-start(), calls=%async_computation.23 | async-start | bytes 1474560 | tf_op jit(solution)/shard_map/reduce_scatter | solution.py:243
  376.3 391.2 %reduce-scatter.30.cloned.1.call-start = ((), (), s32[]{:S(2)}) async-start(), calls=%async_computation.24 | async-start | bytes 1474560 | tf_op jit(solution)/shard_map/reduce_scatter | solution.py:244
  378.0 122.6 %copy-start.63 = (f32[80,256]{1,0:T(8,128)S(1)}, f32[80,256]{1,0:T(8,128)}, u32[]{:S(2)}) copy-start(f32[80,256]{1,0:T(8,128)} %param.46) | copy-start | bytes 245764
  378.0 122.6 %copy-start.64 = (f32[80,256]{1,0:T(8,128)S(1)}, f32[80,256]{1,0:T(8,128)}, u32[]{:S(2)}) copy-start(f32[80,256]{1,0:T(8,128)} %param.45) | copy-start | bytes 245764
  378.0 457.6 %reduce-scatter.32.cloned.1.call-start = ((), (), s32[]{:S(2)}) async-start(), calls=%async_computation.25 | async-start | bytes 1474560 | tf_op jit(solution)/shard_map/reduce_scatter | solution.py:245
  379.7 186.3 %copy-start.65 = (f32[80,256]{1,0:T(8,128)S(1)}, f32[80,256]{1,0:T(8,128)}, u32[]{:S(2)}) copy-start(f32[80,256]{1,0:T(8,128)} %param.44) | copy-start | bytes 245764
  379.7 251.8 %copy-start.66 = (f32[80,256]{1,0:T(8,128)S(1)}, f32[80,256]{1,0:T(8,128)}, u32[]{:S(2)}) copy-start(f32[80,256]{1,0:T(8,128)} %param.47) | copy-start | bytes 245764
  379.7 319.9 %copy-start.60 = (f32[80,512]{1,0:T(8,128)S(1)}, f32[80,512]{1,0:T(8,128)}, u32[]{:S(2)}) copy-start(f32[80,512]{1,0:T(8,128)} %param.48) | copy-start | bytes 491524
  502.2 265.3 %copy-start.61 = (f32[80,512]{1,0:T(8,128)S(1)}, f32[80,512]{1,0:T(8,128)}, u32[]{:S(2)}) copy-start(f32[80,512]{1,0:T(8,128)} %param.49) | copy-start | bytes 491524
  567.5 268.1 %copy-start.62 = (f32[80,512]{1,0:T(8,128)S(1)}, f32[80,512]{1,0:T(8,128)}, u32[]{:S(2)}) copy-start(f32[80,512]{1,0:T(8,128)} %param.50) | copy-start | bytes 491524
  837.2 19.1 %all-to-all-start = ((bf16[8,80,512]{2,1,0:T(8,128)(2,1)}), bf16[8,80,512]{2,1,0:T(8,128)(2,1)S(1)}, u32[]{:S(2)}, u32[]{:S(2)}) async-start(bf16[8,80,512]{2,1,0:T(8,128)(2,1)} %get-tuple-element.128), calls=%async_computation.9 | async-start | bytes 1310720 | tf_op jit(solution)/shard_map/all_to_all | solution.py:268
  840.8 39.8 %reduce-scatter.34.cloned.1.call-start = ((), (), s32[]{:S(2)}) async-start(), calls=%async_computation.26 | async-start | bytes 1024000 | tf_op jit(solution)/shard_map/reduce_scatter | solution.py:68
  858.0 64.0 %reduce-scatter.36.cloned.1.call-start = ((), (), s32[]{:S(2)}) async-start(), calls=%async_computation.27 | async-start | bytes 1024000 | tf_op jit(solution)/shard_map/reduce_scatter | solution.py:68
  897.8 59.9 %reduce-scatter.38.cloned.1.call-start = ((), (), s32[]{:S(2)}) async-start(), calls=%async_computation.28 | async-start | bytes 1024000 | tf_op jit(solution)/shard_map/reduce_scatter | solution.py:68
  933.6 59.7 %reduce-scatter.40.cloned.1.call-start = ((), (), s32[]{:S(2)}) async-start(), calls=%async_computation.29 | async-start | bytes 1024000 | tf_op jit(solution)/shard_map/reduce_scatter | solution.py:68
  969.2 59.7 %reduce-scatter.42.cloned.1.call-start = ((), (), s32[]{:S(2)}) async-start(), calls=%async_computation.30 | async-start | bytes 1024000 | tf_op jit(solution)/shard_map/reduce_scatter | solution.py:68
  1004.8 48.9 %reduce-scatter.22.cloned.1.call-start = ((), (), s32[]{:S(2)}) async-start(), calls=%async_computation.20 | async-start | bytes 819200 | tf_op jit(solution)/shard_map/reduce_scatter | solution.py:58
  1008.1 71.5 %reduce-scatter.44.cloned.1.call-start = ((), (), s32[]{:S(2)}) async-start(), calls=%async_computation.31 | async-start | bytes 1024000 | tf_op jit(solution)/shard_map/reduce_scatter | solution.py:68
  1038.8 15.0 %copy-start.1 = (f32[128,640]{1,0:T(8,128)S(1)}, f32[128,640]{1,0:T(8,128)}, u32[]{:S(2)}) copy-start(f32[128,640]{1,0:T(8,128)} %param.34) | copy-start | bytes 983044
  1090.3 5.8 copy-start.74
  1090.3 46.8 %copy-start.76 = (f32[128]{0:T(128)S(1)}, f32[128]{0:T(128)}, u32[]{:S(2)}) copy-start(f32[128]{0:T(128)} %copy-done.75) | copy-start | bytes 1540
  1090.3 46.8 %copy-start.67 = (f32[3072]{0:T(1024)S(1)}, f32[3072]{0:T(1024)}, u32[]{:S(2)}) copy-start(f32[3072]{0:T(1024)} %param.51) | copy-start | bytes 36868
  1090.3 46.8 %copy-start.69 = (f32[3072]{0:T(1024)S(1)}, f32[3072]{0:T(1024)}, u32[]{:S(2)}) copy-start(f32[3072]{0:T(1024)} %param.52) | copy-start | bytes 36868
  1090.3 46.8 %copy-start.70 = (f32[3072]{0:T(1024)S(1)}, f32[3072]{0:T(1024)}, u32[]{:S(2)}) copy-start(f32[3072]{0:T(1024)} %param.53) | copy-start | bytes 36868
  1090.3 47.5 %copy-start.15 = (f32[128,640]{1,0:T(8,128)S(1)}, f32[128,640]{1,0:T(8,128)}, u32[]{:S(2)}) copy-start(f32[128,640]{1,0:T(8,128)} %copy-done.14) | copy-start | bytes 983044
  1090.3 47.5 %copy-start.50 = (bf16[128,640]{1,0:T(8,128)(2,1)S(1)}, bf16[128,640]{1,0:T(8,128)(2,1)}, u32[]{:S(2)}) copy-start(bf16[128,640]{1,0:T(8,128)(2,1)} %reduce-scatter.22.cloned.1.call-done) | copy-start | bytes 491524
  1090.3 48.3 %copy-start.47 = (f32[80,512]{1,0:T(8,128)S(1)}, f32[80,512]{1,0:T(8,128)}, u32[]{:S(2)}) copy-start(f32[80,512]{1,0:T(8,128)} %param.41) | copy-start | bytes 491524
  1090.3 48.3 %copy-start.48 = (f32[80,512]{1,0:T(8,128)S(1)}, f32[80,512]{1,0:T(8,128)}, u32[]{:S(2)}) copy-start(f32[80,512]{1,0:T(8,128)} %param.42) | copy-start | bytes 491524
  1090.3 48.3 %copy-start.49 = (f32[80,512]{1,0:T(8,128)S(1)}, f32[80,512]{1,0:T(8,128)}, u32[]{:S(2)}) copy-start(f32[80,512]{1,0:T(8,128)} %param.43) | copy-start | bytes 491524
  1090.4 48.3 %all-to-all-start.1 = ((bf16[8,80,512]{2,1,0:T(8,128)(2,1)}), bf16[8,80,512]{2,1,0:T(8,128)(2,1)S(1)}, u32[]{:S(2)}, u32[]{:S(2)}) async-start(bf16[8,80,512]{2,1,0:T(8,128)(2,1)} %bitcast.48), calls=%async_computation.16 | async-start | bytes 1310720 | tf_op jit(solution)/shard_map/all_to_all | solution.py:279
  1096.0 43.5 %copy-start.55 = (f32[80,256]{1,0:T(8,128)S(1)}, f32[80,256]{1,0:T(8,128)}, u32[]{:S(2)}) copy-start(f32[80,256]{1,0:T(8,128)} %param.37) | copy-start | bytes 245764
  1096.0 43.4 %copy-start.57 = (f32[80,256]{1,0:T(8,128)S(1)}, f32[80,256]{1,0:T(8,128)}, u32[]{:S(2)}) copy-start(f32[80,256]{1,0:T(8,128)} %param.38) | copy-start | bytes 245764
  1096.0 43.4 %copy-start.59 = (f32[80,256]{1,0:T(8,128)S(1)}, f32[80,256]{1,0:T(8,128)}, u32[]{:S(2)}) copy-start(f32[80,256]{1,0:T(8,128)} %param.40) | copy-start | bytes 245764
  1137.1 3.1 copy-start.68
  (33 other events, 36.2 us)
Sparse Core Ops, SparseCore 0:
  154.6 22.7 reduce-scatter.15
  274.2 23.0 reduce-scatter.17
  313.9 22.9 reduce-scatter.19
  367.8 132.6 all-reduce.11
  504.2 61.6 reduce-scatter.23
  569.6 61.7 reduce-scatter.25
  635.4 64.1 reduce-scatter.27
  703.5 63.9 reduce-scatter.29
  771.5 64.0 reduce-scatter.31
  858.1 22.4 reduce-scatter.33
  897.9 23.9 reduce-scatter.35
  933.7 23.9 reduce-scatter.37
  969.3 23.9 reduce-scatter.39
  1004.9 23.9 reduce-scatter.41
  1031.3 22.3 reduce-scatter.21
  1056.1 23.4 reduce-scatter.43
where the time goes:
time: 1150 us
  waiting for transfers between devices  661 us (57%)
  blocking collectives  349 us (30%)
  matrix products  49.4 us (4%)
  other arithmetic  43.5 us (4%)
  local copies, waits for them, and re-layouts  19 us (2%)
  between operations  15.7 us (1%)
    reduce_scatter x6, waiting for transfers between devices, gram_whole(): lax.psum_scatter(gram_part.astype(jnp.bfloat16), 'tensor', scatter_dimens...  140 us
    psum x1, waiting for transfers between devices, body(): lax.psum((grad_key_part, grad_value_part, gain_term), ('dp', 'tensor'))  121 us
    reduce_scatter x1, waiting for transfers between devices, body(): lax.psum_scatter(grad_down_part, 'dp', scatter_dimension=0, tiled=True)  66.4 us
    reduce_scatter x1, waiting for transfers between devices, body(): lax.psum_scatter(grad_up_part, 'dp', scatter_dimension=0, tiled=True)  66.3 us
    reduce_scatter x1, waiting for transfers between devices, body(): lax.psum_scatter(grad_gate_part, 'dp', scatter_dimension=0, tiled=True)  65.9 us
    reduce_scatter x1, waiting for transfers between devices, body(): lax.psum_scatter(grad_query_part, 'dp', scatter_dimension=0, tiled=True)  63.7 us
    reduce_scatter x1, waiting for transfers between devices, body(): lax.psum_scatter(grad_output_part, 'dp', scatter_dimension=0, tiled=True)  61.8 us
    reduce_scatter x4, waiting for transfers between devices, sum_rows(): lax.psum_scatter(term(jnp.int32(0), rows * lax.axis_size('tensor')).astyp...  59.6 us
  transfers between devices with their start and end apart: 18, of which 16 were waited for; matrix products, arithmetic and copies ran while one was open for 3% of the time, Pallas kernels for 0%

commit v1 on v0

--- a/solution.py
+++ b/solution.py
@@ -245,7 +245,7 @@
         lax.psum_scatter(grad_down_part, "dp", scatter_dimension=0, tiled=True),
     )
     key_total, value_total, grad_gains = lax.psum(
-        (grad_key_part, grad_value_part, gain_term), ("dp", "tensor")
+        lax.psum((grad_key_part, grad_value_part, gain_term), "tensor"), "dp"
     )
     shard_rows = w_key.shape[0]
     my_data = lax.axis_index("dp")

time: 1150 us -> 1150 us (level)
    psum x1 -> x2, blocking collectives: 41 us -> 48.7 us  [the longest x1 37.4 us: body(): lax.psum(lax.psum((grad_key_part, grad_value_part, gain_term), 'tensor'),...]
    psum x1 -> x2, waiting for transfers between devices: 121 us -> 118 us  [the longest x1 84.9 us: body(): lax.psum(lax.psum((grad_key_part, grad_value_part, gain_term), 'tensor'),...]
  transfers between devices with their start and end apart: 18 -> 19, of which waited for: 16 -> 17; matrix products, arithmetic and copies ran while one was open for 3% -> 3% of each run, Pallas kernels for 0% -> 0%
where the time goes in v1:
time: 1150 us
  waiting for transfers between devices  655 us (57%)
  blocking collectives  357 us (31%)
  matrix products  49.4 us (4%)
  other arithmetic  43.5 us (4%)
  local copies, waits for them, and re-layouts  19 us (2%)
  between operations  15.7 us (1%)
    reduce_scatter x6, waiting for transfers between devices, gram_whole(): lax.psum_scatter(gram_part.astype(jnp.bfloat16), 'tensor', scatter_dimens...  140 us
    psum x1, waiting for transfers between devices, body(): lax.psum(lax.psum((grad_key_part, grad_value_part, gain_term), 'tensor'),...  84.9 us
    reduce_scatter x1, waiting for transfers between devices, body(): lax.psum_scatter(grad_up_part, 'dp', scatter_dimension=0, tiled=True)  66.6 us
    reduce_scatter x1, waiting for transfers between devices, body(): lax.psum_scatter(grad_down_part, 'dp', scatter_dimension=0, tiled=True)  66.4 us
    reduce_scatter x1, waiting for transfers between devices, body(): lax.psum_scatter(grad_gate_part, 'dp', scatter_dimension=0, tiled=True)  64.6 us
    reduce_scatter x1, waiting for transfers between devices, body(): lax.psum_scatter(grad_output_part, 'dp', scatter_dimension=0, tiled=True)  63 us
    reduce_scatter x1, waiting for transfers between devices, body(): lax.psum_scatter(grad_query_part, 'dp', scatter_dimension=0, tiled=True)  61.3 us
    reduce_scatter x4, waiting for transfers between devices, sum_rows(): lax.psum_scatter(term(jnp.int32(0), rows * lax.axis_size('tensor')).astyp...  59.4 us
  transfers between devices with their start and end apart: 19, of which 17 were waited for; matrix products, arithmetic and copies ran while one was open for 3% of the time, Pallas kernels for 0%

profile of v1, /device:TPU:0, one launch (start us, length us, event | category | flops | bytes accessed | tf_op | source)
XLA Modules:
  0.0 1149.2 jit_solution(7139461176965732375)
XLA Ops:
  11.0 9.4 all_gather.51
  20.4 31.4 %all_gather.53 = bf16[640,256]{1,0:T(8,128)(2,1)S(1)} all-gather(bf16[80,256]{1,0:T(8,128)(2,1)S(1)} %convert_element_type.303), channel_id=1, replica_groups=mesh['dp'=8,'tensor'=4] {'dp'}, dimensions={0}, use_global_device_ids=true | all-gather | bytes 368640 | tf_op jit(solution)/shard_map/all_gather | solution.py:127
  53.1 30.8 %all_gather.54 = bf16[640,256]{1,0:T(8,128)(2,1)S(1)} all-gather(bf16[80,256]{1,0:T(8,128)(2,1)S(1)} %convert_element_type.307), channel_id=1, replica_groups=mesh['dp'=8,'tensor'=4] {'dp'}, dimensions={0}, use_global_device_ids=true | all-gather | bytes 368640 | tf_op jit(solution)/shard_map/all_gather | solution.py:126
  86.3 2.5 fusion.43
  89.8 31.0 %all_gather.52 = bf16[640,256]{1,0:T(8,128)(2,1)S(1)} all-gather(bf16[80,256]{1,0:T(8,128)(2,1)S(1)} %convert_element_type.301), channel_id=1, replica_groups=mesh['dp'=8,'tensor'=4] {'dp'}, dimensions={0}, use_global_device_ids=true | all-gather | bytes 368640 | tf_op jit(solution)/shard_map/all_gather | solution.py:128
  121.6 31.3 %all_gather.55 = bf16[640,256]{1,0:T(8,128)(2,1)S(1)} all-gather(bf16[80,256]{1,0:T(8,128)(2,1)S(1)} %convert_element_type.313), channel_id=1, replica_groups=mesh['dp'=8,'tensor'=4] {'dp'}, dimensions={0}, use_global_device_ids=true | all-gather | bytes 368640 | tf_op jit(solution)/shard_map/all_gather | solution.py:129
  157.4 34.0 %all_gather.57 = bf16[640,512]{1,0:T(8,128)(2,1)} all-gather(bf16[80,512]{1,0:T(8,128)(2,1)S(1)} %convert_element_type.317), channel_id=1, replica_groups=mesh['dp'=8,'tensor'=4] {'dp'}, dimensions={0}, use_global_device_ids=true | all-gather | bytes 737280 | tf_op jit(solution)/shard_map/all_gather | solution.py:130
  191.4 33.7 %all_gather.58 = bf16[640,512]{1,0:T(8,128)(2,1)} all-gather(bf16[80,512]{1,0:T(8,128)(2,1)S(1)} %convert_element_type.318), channel_id=1, replica_groups=mesh['dp'=8,'tensor'=4] {'dp'}, dimensions={0}, use_global_device_ids=true | all-gather | bytes 737280 | tf_op jit(solution)/shard_map/all_gather | solution.py:131
  225.1 33.4 %all_gather.59 = bf16[640,512]{1,0:T(8,128)(2,1)} all-gather(bf16[80,512]{1,0:T(8,128)(2,1)S(1)} %convert_element_type.320), channel_id=1, replica_groups=mesh['dp'=8,'tensor'=4] {'dp'}, dimensions={0}, use_global_device_ids=true | all-gather | bytes 737280 | tf_op jit(solution)/shard_map/all_gather | solution.py:132
  261.6 7.6 all_gather.56
  270.2 1.7 multiply_convert_fusion.7
  274.3 23.0 %reduce-scatter.18.cloned.1.call-done = bf16[128,640]{1,0:T(8,128)(2,1)} async-done(((bf16[512,640]{1,0:T(8,128)(2,1)}), bf16[128,640]{1,0:T(8,128)(2,1)}) %reduce-scatter.18.cloned.1.call-update) | async-done | bytes 163856 | tf_op jit(solution)/shard_map/reduce_scatter | solution.py:58
  300.8 7.3 all_gather.60
  308.2 2.7 multiply_convert_fusion.6
  313.9 23.1 %reduce-scatter.20.cloned.1.call-done = bf16[128,640]{1,0:T(8,128)(2,1)} async-done(((bf16[512,640]{1,0:T(8,128)(2,1)}), bf16[128,640]{1,0:T(8,128)(2,1)}) %reduce-scatter.20.cloned.1.call-update) | async-done | bytes 163856 | tf_op jit(solution)/shard_map/reduce_scatter | solution.py:58
  338.9 2.3 fusion.71
  342.0 7.5 all_gather.61
  352.5 1.9 copy.50
  354.4 2.3 fusion.130
  357.8 1.9 fusion.55
  359.8 2.2 fusion.56
  363.4 3.5 fusion.49
  368.1 3.6 fusion.57
  374.6 33.0 %all-reduce.16.cloned.1.call-done = (f32[640,256]{1,0:T(8,128)}, f32[640,256]{1,0:T(8,128)}) async-done(((f32[640,256]{1,0:T(8,128)}, f32[640,256]{1,0:T(8,128)}), (f32[640,256]{1,0:T(8,128)}, f32[640,256]{1,0:T(8,128)})) %all-reduce.16.cloned.1.call-update) | async-done | bytes 1310736 | tf_op jit(solution)/shard_map/psum | solution.py:248
  407.7 1.6 fusion.132
  409.4 1.6 fusion.133
  411.1 1.6 fusion.134
  412.8 61.3 %reduce-scatter.24.cloned.1.call-done = f32[80,256]{1,0:T(8,128)} async-done(((f32[640,256]{1,0:T(8,128)}), f32[80,256]{1,0:T(8,128)}) %reduce-scatter.24.cloned.1.call-update) | async-done | bytes 81936 | tf_op jit(solution)/shard_map/reduce_scatter | solution.py:241
  474.1 1.5 add_convert_fusion.6
  476.5 63.0 %reduce-scatter.26.cloned.1.call-done = f32[80,256]{1,0:T(8,128)} async-done(((f32[640,256]{1,0:T(8,128)}), f32[80,256]{1,0:T(8,128)}) %reduce-scatter.26.cloned.1.call-update) | async-done | bytes 81936 | tf_op jit(solution)/shard_map/reduce_scatter | solution.py:242
  541.1 84.9 %all-reduce.14.cloned.1.call-done = (f32[640,256]{1,0:T(8,128)}, f32[640,256]{1,0:T(8,128)}) async-done(((f32[640,256]{1,0:T(8,128)}, f32[640,256]{1,0:T(8,128)}), (f32[640,256]{1,0:T(8,128)}, f32[640,256]{1,0:T(8,128)})) %all-reduce.14.cloned.1.call-update) | async-done | bytes 1310736 | tf_op jit(solution)/shard_map/psum | solution.py:247
  626.0 1.7 add_convert_fusion.4
  629.5 64.6 %reduce-scatter.28.cloned.1.call-done = f32[80,512]{1,0:T(8,128)} async-done(((f32[640,512]{1,0:T(8,128)}), f32[80,512]{1,0:T(8,128)}) %reduce-scatter.28.cloned.1.call-update) | async-done | bytes 163856 | tf_op jit(solution)/shard_map/reduce_scatter | solution.py:243
  694.1 1.6 fusion.97
  695.7 66.6 %reduce-scatter.30.cloned.1.call-done = f32[80,512]{1,0:T(8,128)} async-done(((f32[640,512]{1,0:T(8,128)}), f32[80,512]{1,0:T(8,128)}) %reduce-scatter.30.cloned.1.call-update) | async-done | bytes 163856 | tf_op jit(solution)/shard_map/reduce_scatter | solution.py:244
  762.3 1.6 fusion.99
  763.9 66.4 %reduce-scatter.32.cloned.1.call-done = f32[80,512]{1,0:T(8,128)} async-done(((f32[640,512]{1,0:T(8,128)}), f32[80,512]{1,0:T(8,128)}) %reduce-scatter.32.cloned.1.call-update) | async-done | bytes 163856 | tf_op jit(solution)/shard_map/reduce_scatter | solution.py:245
  830.3 1.6 fusion.101
  832.0 3.5 all-to-all-start
  835.6 15.5 %all-to-all-done = bf16[8,80,512]{2,1,0:T(8,128)(2,1)S(1)} async-done(((bf16[8,80,512]{2,1,0:T(8,128)(2,1)}), bf16[8,80,512]{2,1,0:T(8,128)(2,1)S(1)}, u32[]{:S(2)}, u32[]{:S(2)}) %all-to-all-start) | async-done | bytes 655392 | tf_op jit(solution)/shard_map/all_to_all | solution.py:268
  851.1 1.6 multiply_convert_fusion.5
  852.8 22.5 %reduce-scatter.34.cloned.1.call-done = bf16[160,640]{1,0:T(8,128)(2,1)} async-done(((bf16[640,640]{1,0:T(8,128)(2,1)}), bf16[160,640]{1,0:T(8,128)(2,1)}) %reduce-scatter.34.cloned.1.call-update) | async-done | bytes 204816 | tf_op jit(solution)/shard_map/reduce_scatter | solution.py:68
  875.3 8.4 all_gather.62
  883.7 5.8 gather_fusion
  890.9 1.6 multiply_convert_fusion.4
  892.7 23.9 %reduce-scatter.36.cloned.1.call-done = bf16[160,640]{1,0:T(8,128)(2,1)} async-done(((bf16[640,640]{1,0:T(8,128)(2,1)}), bf16[160,640]{1,0:T(8,128)(2,1)}) %reduce-scatter.36.cloned.1.call-update) | async-done | bytes 204816 | tf_op jit(solution)/shard_map/reduce_scatter | solution.py:68
  916.6 8.6 all_gather.63
  926.7 1.6 multiply_convert_fusion.3
  928.4 24.0 %reduce-scatter.38.cloned.1.call-done = bf16[160,640]{1,0:T(8,128)(2,1)} async-done(((bf16[640,640]{1,0:T(8,128)(2,1)}), bf16[160,640]{1,0:T(8,128)(2,1)}) %reduce-scatter.38.cloned.1.call-update) | async-done | bytes 204816 | tf_op jit(solution)/shard_map/reduce_scatter | solution.py:68
  952.4 8.4 all_gather.64
  962.3 1.6 multiply_convert_fusion.2
  963.9 24.1 %reduce-scatter.40.cloned.1.call-done = bf16[160,640]{1,0:T(8,128)(2,1)} async-done(((bf16[640,640]{1,0:T(8,128)(2,1)}), bf16[160,640]{1,0:T(8,128)(2,1)}) %reduce-scatter.40.cloned.1.call-update) | async-done | bytes 204816 | tf_op jit(solution)/shard_map/reduce_scatter | solution.py:68
  988.0 8.4 all_gather.65
  997.9 1.6 multiply_convert_fusion.1
  1002.9 20.8 %reduce-scatter.42.cloned.1.call-done = bf16[160,640]{1,0:T(8,128)(2,1)} async-done(((bf16[640,640]{1,0:T(8,128)(2,1)}), bf16[160,640]{1,0:T(8,128)(2,1)}) %reduce-scatter.42.cloned.1.call-update) | async-done | bytes 204816 | tf_op jit(solution)/shard_map/reduce_scatter | solution.py:68
  1023.6 8.4 all_gather.66
  1033.5 1.6 multiply_convert_fusion
  1035.1 13.3 %reduce-scatter.22.cloned.1.call-done = bf16[128,640]{1,0:T(8,128)(2,1)} async-done(((bf16[512,640]{1,0:T(8,128)(2,1)}), bf16[128,640]{1,0:T(8,128)(2,1)}) %reduce-scatter.22.cloned.1.call-update) | async-done | bytes 163856 | tf_op jit(solution)/shard_map/reduce_scatter | solution.py:58
  1049.5 24.8 %reduce-scatter.44.cloned.1.call-done = bf16[160,640]{1,0:T(8,128)(2,1)} async-done(((bf16[640,640]{1,0:T(8,128)(2,1)}), bf16[160,640]{1,0:T(8,128)(2,1)}) %reduce-scatter.44.cloned.1.call-update) | async-done | bytes 204816 | tf_op jit(solution)/shard_map/reduce_scatter | solution.py:68
  1074.3 8.4 all_gather.67
  1083.4 1.6 fusion.12
  1085.1 5.6 all-to-all-start.1
  1090.8 11.3 psum.46
  1102.1 37.4 %psum.47 = f32[3072]{0:T(1024)S(1)} all-reduce(f32[3072]{0:T(1024)S(1)} %psum.46), channel_id=1, replica_groups=mesh['dp'=8,'tensor'=4] {'dp'}, use_global_device_ids=true, to_apply=%region_35.36 | all-reduce | flops 3072 | bytes 24576 | tf_op jit(solution)/shard_map/psum | solution.py:247
  (290 shorter events, 58.5 us)
Async XLA Ops:
  7.2 13.2 %copy-start.56 = (f32[80,256]{1,0:T(8,128)S(1)}, f32[80,256]{1,0:T(8,128)}, u32[]{:S(2)}) copy-start(f32[80,256]{1,0:T(8,128)} %param.38) | copy-start | bytes 245764
  7.2 251.3 %reduce-scatter.16.cloned.1.call-start = ((), (), s32[]{:S(2)}) async-start(), calls=%async_computation.17 | async-start | bytes 819200 | tf_op jit(solution)/shard_map/reduce_scatter | solution.py:58
  9.9 42.3 %copy-start.75 = (f32[128]{0:T(128)}, f32[128]{0:T(128)S(1)}, u32[]{:S(2)}) copy-start(f32[128]{0:T(128)S(1)} %multiply_reduce_fusion.4) | copy-start | bytes 1540
  89.2 32.0 %copy-start.58 = (f32[80,256]{1,0:T(8,128)S(1)}, f32[80,256]{1,0:T(8,128)}, u32[]{:S(2)}) copy-start(f32[80,256]{1,0:T(8,128)} %param.40) | copy-start | bytes 245764
  121.2 31.6 %copy-start.30 = (bf16[512,256]{1,0:T(8,128)(2,1)}, bf16[512,256]{1,0:T(8,128)(2,1)S(1)}, u32[]{:S(2)}) copy-start(bf16[512,256]{1,0:T(8,128)(2,1)S(1)} %convolution_convert_fusion.10) | copy-start | bytes 786436
  154.5 142.8 %reduce-scatter.18.cloned.1.call-start = ((), (), s32[]{:S(2)}) async-start(), calls=%async_computation.18 | async-start | bytes 819200 | tf_op jit(solution)/shard_map/reduce_scatter | solution.py:58
  156.4 103.2 %copy-start = (f32[128,640]{1,0:T(8,128)S(1)}, f32[128,640]{1,0:T(8,128)}, u32[]{:S(2)}) copy-start(f32[128,640]{1,0:T(8,128)} %param.34) | copy-start | bytes 983044
  258.5 10.7 copy-start.4
  259.6 10.1 copy-start.77
  260.7 9.0 copy-start.78
  260.8 76.2 %copy-start.72 = (f32[128]{0:T(128)}, f32[128]{0:T(128)S(1)}, u32[]{:S(2)}) copy-start(f32[128]{0:T(128)S(1)} %fusion.115) | copy-start | bytes 1540
  270.2 2.5 copy-start.45
  274.2 62.8 %reduce-scatter.20.cloned.1.call-start = ((), (), s32[]{:S(2)}) async-start(), calls=%async_computation.19 | async-start | bytes 819200 | tf_op jit(solution)/shard_map/reduce_scatter | solution.py:58
  297.3 10.9 copy-start.41
  297.3 10.9 copy-start.46
  298.4 12.4 %copy-start.73 = (f32[128]{0:T(128)}, f32[128]{0:T(128)S(1)}, u32[]{:S(2)}) copy-start(f32[128]{0:T(128)S(1)} %fusion.116) | copy-start | bytes 1540
  308.2 2.7 copy-start.25
  308.2 2.7 copy-start.5
  313.8 93.8 %all-reduce.16.cloned.1.call-start = ((), (), s32[]{:S(2)}) async-start(), calls=%async_computation.33 | async-start | bytes 2621440 | tf_op jit(solution)/shard_map/psum | solution.py:248
  337.0 4.9 copy-start.24
  338.9 11.5 %copy-start.21 = (bf16[640,256]{1,0:T(8,128)(2,1)S(1)}, bf16[640,256]{1,0:T(8,128)(2,1)}, u32[]{:S(2)}) copy-start(bf16[640,256]{1,0:T(8,128)(2,1)} %copy-done.20) | copy-start | bytes 983044
  354.4 2.3 copy-start.10
  354.4 2.3 copy-start.36
  354.4 2.4 copy-start.13
  354.4 2.4 copy-start.31
  357.2 2.5 copy-start.7
  367.8 106.3 %reduce-scatter.24.cloned.1.call-start = ((), (), s32[]{:S(2)}) async-start(), calls=%async_computation.21 | async-start | bytes 737280 | tf_op jit(solution)/shard_map/reduce_scatter | solution.py:241
  373.2 166.3 %reduce-scatter.26.cloned.1.call-start = ((), (), s32[]{:S(2)}) async-start(), calls=%async_computation.22 | async-start | bytes 737280 | tf_op jit(solution)/shard_map/reduce_scatter | solution.py:242
  374.5 33.2 %copy-start.35 = (bf16[512,512]{1,0:T(8,128)(2,1)S(1)}, bf16[512,512]{1,0:T(8,128)(2,1)}, u32[]{:S(2)}) copy-start(bf16[512,512]{1,0:T(8,128)(2,1)} %copy-done.34) | copy-start | bytes 1572868
  374.6 251.4 %all-reduce.14.cloned.1.call-start = ((), (), s32[]{:S(2)}) async-start(), calls=%async_computation.32 | async-start | bytes 2621440 | tf_op jit(solution)/shard_map/psum | solution.py:247
  407.6 286.5 %reduce-scatter.28.cloned.1.call-start = ((), (), s32[]{:S(2)}) async-start(), calls=%async_computation.23 | async-start | bytes 1474560 | tf_op jit(solution)/shard_map/reduce_scatter | solution.py:243
  409.3 352.9 %reduce-scatter.30.cloned.1.call-start = ((), (), s32[]{:S(2)}) async-start(), calls=%async_computation.24 | async-start | bytes 1474560 | tf_op jit(solution)/shard_map/reduce_scatter | solution.py:244
  411.0 63.1 %copy-start.65 = (f32[80,256]{1,0:T(8,128)S(1)}, f32[80,256]{1,0:T(8,128)}, u32[]{:S(2)}) copy-start(f32[80,256]{1,0:T(8,128)} %param.44) | copy-start | bytes 245764
  411.0 419.3 %reduce-scatter.32.cloned.1.call-start = ((), (), s32[]{:S(2)}) async-start(), calls=%async_computation.25 | async-start | bytes 1474560 | tf_op jit(solution)/shard_map/reduce_scatter | solution.py:245
  412.7 126.8 %copy-start.66 = (f32[80,256]{1,0:T(8,128)S(1)}, f32[80,256]{1,0:T(8,128)}, u32[]{:S(2)}) copy-start(f32[80,256]{1,0:T(8,128)} %param.47) | copy-start | bytes 245764
  412.7 213.3 %copy-start.63 = (f32[80,256]{1,0:T(8,128)S(1)}, f32[80,256]{1,0:T(8,128)}, u32[]{:S(2)}) copy-start(f32[80,256]{1,0:T(8,128)} %param.46) | copy-start | bytes 245764
  412.7 213.3 %copy-start.64 = (f32[80,256]{1,0:T(8,128)S(1)}, f32[80,256]{1,0:T(8,128)}, u32[]{:S(2)}) copy-start(f32[80,256]{1,0:T(8,128)} %param.45) | copy-start | bytes 245764
  412.7 281.4 %copy-start.60 = (f32[80,512]{1,0:T(8,128)S(1)}, f32[80,512]{1,0:T(8,128)}, u32[]{:S(2)}) copy-start(f32[80,512]{1,0:T(8,128)} %param.48) | copy-start | bytes 491524
  475.6 286.6 %copy-start.61 = (f32[80,512]{1,0:T(8,128)S(1)}, f32[80,512]{1,0:T(8,128)}, u32[]{:S(2)}) copy-start(f32[80,512]{1,0:T(8,128)} %param.49) | copy-start | bytes 491524
  476.5 353.8 %copy-start.62 = (f32[80,512]{1,0:T(8,128)S(1)}, f32[80,512]{1,0:T(8,128)}, u32[]{:S(2)}) copy-start(f32[80,512]{1,0:T(8,128)} %param.50) | copy-start | bytes 491524
  832.0 19.1 %all-to-all-start = ((bf16[8,80,512]{2,1,0:T(8,128)(2,1)}), bf16[8,80,512]{2,1,0:T(8,128)(2,1)S(1)}, u32[]{:S(2)}, u32[]{:S(2)}) async-start(bf16[8,80,512]{2,1,0:T(8,128)(2,1)} %get-tuple-element.130), calls=%async_computation.9 | async-start | bytes 1310720 | tf_op jit(solution)/shard_map/all_to_all | solution.py:268
  835.5 39.8 %reduce-scatter.34.cloned.1.call-start = ((), (), s32[]{:S(2)}) async-start(), calls=%async_computation.26 | async-start | bytes 1024000 | tf_op jit(solution)/shard_map/reduce_scatter | solution.py:68
  852.7 63.9 %reduce-scatter.36.cloned.1.call-start = ((), (), s32[]{:S(2)}) async-start(), calls=%async_computation.27 | async-start | bytes 1024000 | tf_op jit(solution)/shard_map/reduce_scatter | solution.py:68
  892.5 59.9 %reduce-scatter.38.cloned.1.call-start = ((), (), s32[]{:S(2)}) async-start(), calls=%async_computation.28 | async-start | bytes 1024000 | tf_op jit(solution)/shard_map/reduce_scatter | solution.py:68
  928.3 59.7 %reduce-scatter.40.cloned.1.call-start = ((), (), s32[]{:S(2)}) async-start(), calls=%async_computation.29 | async-start | bytes 1024000 | tf_op jit(solution)/shard_map/reduce_scatter | solution.py:68
  963.9 59.7 %reduce-scatter.42.cloned.1.call-start = ((), (), s32[]{:S(2)}) async-start(), calls=%async_computation.30 | async-start | bytes 1024000 | tf_op jit(solution)/shard_map/reduce_scatter | solution.py:68
  999.5 48.9 %reduce-scatter.22.cloned.1.call-start = ((), (), s32[]{:S(2)}) async-start(), calls=%async_computation.20 | async-start | bytes 819200 | tf_op jit(solution)/shard_map/reduce_scatter | solution.py:58
  1002.8 71.5 %reduce-scatter.44.cloned.1.call-start = ((), (), s32[]{:S(2)}) async-start(), calls=%async_computation.31 | async-start | bytes 1024000 | tf_op jit(solution)/shard_map/reduce_scatter | solution.py:68
  1033.5 15.0 %copy-start.1 = (f32[128,640]{1,0:T(8,128)S(1)}, f32[128,640]{1,0:T(8,128)}, u32[]{:S(2)}) copy-start(f32[128,640]{1,0:T(8,128)} %param.34) | copy-start | bytes 983044
  1085.0 5.8 copy-start.74
  1085.0 54.5 %copy-start.76 = (f32[128]{0:T(128)S(1)}, f32[128]{0:T(128)}, u32[]{:S(2)}) copy-start(f32[128]{0:T(128)} %copy-done.75) | copy-start | bytes 1540
  1085.0 54.5 %copy-start.67 = (f32[3072]{0:T(1024)S(1)}, f32[3072]{0:T(1024)}, u32[]{:S(2)}) copy-start(f32[3072]{0:T(1024)} %param.51) | copy-start | bytes 36868
  1085.0 54.5 %copy-start.69 = (f32[3072]{0:T(1024)S(1)}, f32[3072]{0:T(1024)}, u32[]{:S(2)}) copy-start(f32[3072]{0:T(1024)} %param.52) | copy-start | bytes 36868
  1085.0 54.5 %copy-start.70 = (f32[3072]{0:T(1024)S(1)}, f32[3072]{0:T(1024)}, u32[]{:S(2)}) copy-start(f32[3072]{0:T(1024)} %param.53) | copy-start | bytes 36868
  1085.0 55.2 %copy-start.15 = (f32[128,640]{1,0:T(8,128)S(1)}, f32[128,640]{1,0:T(8,128)}, u32[]{:S(2)}) copy-start(f32[128,640]{1,0:T(8,128)} %copy-done.14) | copy-start | bytes 983044
  1085.1 55.1 %copy-start.50 = (bf16[128,640]{1,0:T(8,128)(2,1)S(1)}, bf16[128,640]{1,0:T(8,128)(2,1)}, u32[]{:S(2)}) copy-start(bf16[128,640]{1,0:T(8,128)(2,1)} %reduce-scatter.22.cloned.1.call-done) | copy-start | bytes 491524
  1085.1 56.0 %copy-start.47 = (f32[80,512]{1,0:T(8,128)S(1)}, f32[80,512]{1,0:T(8,128)}, u32[]{:S(2)}) copy-start(f32[80,512]{1,0:T(8,128)} %param.41) | copy-start | bytes 491524
  1085.1 56.0 %copy-start.48 = (f32[80,512]{1,0:T(8,128)S(1)}, f32[80,512]{1,0:T(8,128)}, u32[]{:S(2)}) copy-start(f32[80,512]{1,0:T(8,128)} %param.42) | copy-start | bytes 491524
  1085.1 56.0 %copy-start.49 = (f32[80,512]{1,0:T(8,128)S(1)}, f32[80,512]{1,0:T(8,128)}, u32[]{:S(2)}) copy-start(f32[80,512]{1,0:T(8,128)} %param.43) | copy-start | bytes 491524
  1085.1 55.9 %all-to-all-start.1 = ((bf16[8,80,512]{2,1,0:T(8,128)(2,1)}), bf16[8,80,512]{2,1,0:T(8,128)(2,1)S(1)}, u32[]{:S(2)}, u32[]{:S(2)}) async-start(bf16[8,80,512]{2,1,0:T(8,128)(2,1)} %bitcast.48), calls=%async_computation.16 | async-start | bytes 1310720 | tf_op jit(solution)/shard_map/all_to_all | solution.py:279
  1090.7 51.1 %copy-start.55 = (f32[80,256]{1,0:T(8,128)S(1)}, f32[80,256]{1,0:T(8,128)}, u32[]{:S(2)}) copy-start(f32[80,256]{1,0:T(8,128)} %param.37) | copy-start | bytes 245764
  1090.8 51.1 %copy-start.57 = (f32[80,256]{1,0:T(8,128)S(1)}, f32[80,256]{1,0:T(8,128)}, u32[]{:S(2)}) copy-start(f32[80,256]{1,0:T(8,128)} %param.38) | copy-start | bytes 245764
  1090.8 51.1 %copy-start.59 = (f32[80,256]{1,0:T(8,128)S(1)}, f32[80,256]{1,0:T(8,128)}, u32[]{:S(2)}) copy-start(f32[80,256]{1,0:T(8,128)} %param.40) | copy-start | bytes 245764
  1139.5 3.1 copy-start.68
  (34 other events, 38.9 us)
Sparse Core Ops, SparseCore 0:
  154.6 22.7 reduce-scatter.15
  274.3 22.8 reduce-scatter.17
  314.0 22.9 reduce-scatter.19
  367.9 39.6 all-reduce.15
  411.3 62.7 reduce-scatter.23
  477.8 61.7 reduce-scatter.25
  543.2 82.7 all-reduce.13
  629.9 64.1 reduce-scatter.27
  698.1 64.1 reduce-scatter.29
  766.1 64.1 reduce-scatter.31
  852.8 22.4 reduce-scatter.33
  892.6 23.9 reduce-scatter.35
  928.4 23.9 reduce-scatter.37
  964.0 23.9 reduce-scatter.39
  999.6 23.9 reduce-scatter.41
  1026.0 22.3 reduce-scatter.21
  1050.8 23.4 reduce-scatter.43
